TPU v7x, 128 devices: a whole 4x4x4 slice. The times are simulated.
128 devices in a mesh: seq: 8 (over x, core), grp: 16 (over z, y).
Axes of the slice: x: 4, y: 4, z: 4, core: 2. Of those that a mesh axis runs over, the one named last changes fastest.
Arguments:
- tokens: bfloat16 [16, 1024, 1536], P('grp', 'seq'), may hold values from -15 to 15
- lengths: int32 [16, 3], P('grp'), may hold values from 1 to 512, 1024 in all within a row
- prompt_adapter: int32 [16, 3], P('grp'), may hold values from 0 to 15
- routes: int32 [16, 1024, 8], P('grp', 'seq'), may hold values from 0 to 39, all different within a row; in each aligned block of 128 rows (0 to 127, 128 to 255, ..., all dimensions but the last counted through in order) at most 40 rows name the same one
- routing_weight: float32 [16, 1024, 8], P('grp', 'seq'), may hold values from 0.1 to 1
- attention_gain: float32 [1536], replicated, may hold values from 0.5 to 1.5
- query_weight: bfloat16 [1536, 1536], replicated, may hold values from -25 to 25
- key_weight: bfloat16 [1536, 512], replicated, may hold values from -0.15625 to 0.15625
- value_weight: bfloat16 [1536, 512], replicated, may hold values from -0.15625 to 0.15625
- output_weight: bfloat16 [1536, 1536], replicated, may hold values from -0.15625 to 0.15625
- adapter_down_maps: bfloat16 [4, 16, 1536, 16], P(None, 'grp'), may hold values from -0.15625 to 0.15625
- adapter_up_query_output: bfloat16 [2, 16, 16, 1536], P(None, 'grp'), may hold values from -1.5 to 1.5
- adapter_up_key_value: bfloat16 [2, 16, 16, 512], P(None, 'grp'), may hold values from -1.5 to 1.5
- expert_gain: float32 [1536], replicated, may hold values from 0.5 to 1.5
- gate_weight: bfloat16 [80, 1536, 256], P('grp'), may hold values from -0.15625 to 0.15625
- up_weight: bfloat16 [80, 1536, 256], P('grp'), may hold values from -0.15625 to 0.15625
- down_weight: bfloat16 [80, 256, 1536], P('grp'), may hold values from -0.25 to 0.25
- closing_gain: float32 [1536], replicated, may hold values from 0.5 to 1.5
- vocab_projection: bfloat16 [1536, 49152], P(None, ('seq', 'grp')), may hold values from -10 to 10
Outputs:
- hidden_out: bfloat16 [16, 1024, 1536], P('grp', 'seq')
- log_probs: float32 [48, 49152], P(None, ('seq', 'grp'))
Inputs may be any that keep to these rules, and one draw needn't show every extreme that they name: The 3 lengths of a group sum to 1024; the longest is exactly 512. `routes`: A token names 8 different experts. Within the 128 tokens of one device no expert is named by more than 40 of them, and in every draw some expert is named by exactly 40 tokens of some device.
All inputs are finite; a program needn't handle non-finite values.
Results may differ from a plain program's by a relative error of at most 0.017.
The roundings to bfloat16 on the way count: a program that leaves them out, or rounds other values in their place, can miss the bound.
Values may be sent and summed in bfloat16 or wider, within the bound.
No kernel may reach another device: no remote copies, remote signals or barrier semaphores. Data moves between devices by JAX's collectives and lax.ppermute only.
A program may use at most 192 MiB of HBM per device.

v0:
```python
import jax
import jax.numpy as jnp
from jax import lax
from jax.sharding import PartitionSpec as P

HEADS = 24
KV_HEADS = 8
HEAD = 64
EXPERTS = 40
TOP = 8
CAP = 40
EPSILON = 1e-05
ROPE_BASE = 10000.0
MASKED = -1e30


def rms_scaled(features, scales):
    features = features.astype(jnp.float32)
    inverse = lax.rsqrt(jnp.mean(features * features, axis=-1, keepdims=True) + EPSILON)
    return (features * inverse * scales).astype(jnp.bfloat16)


def rotate(features, offsets):
    half_size = features.shape[-1] // 2
    frequency = ROPE_BASE ** (-jnp.arange(half_size, dtype=jnp.float32) / half_size)
    angles = offsets.astype(jnp.float32)[:, None, None] * frequency[None, None, :]
    cosine = jnp.cos(angles)
    sines = jnp.sin(angles)
    first_half = features[..., :half_size]
    second = features[..., half_size:]
    return jnp.concatenate(
        [first_half * cosine - second * sines, second * cosine + first_half * sines], axis=-1
    )


def doc_layout(prompt_lens, row_index):
    doc_ends = jnp.cumsum(prompt_lens)
    starts = doc_ends - prompt_lens
    document = jnp.sum((row_index[:, None] >= doc_ends[None, :]).astype(jnp.int32), axis=1)
    member = document[:, None] == jnp.arange(prompt_lens.shape[0], dtype=jnp.int32)[None, :]
    doc_start = jnp.sum(jnp.where(member, starts[None, :], 0), axis=1)
    return (document, row_index - doc_start, member)


def adapter_delta(normalized_rows, selected_experts, down_proj, up_weights):
    low_rank = jnp.einsum(
        "td,adr->tar", normalized_rows, down_proj, preferred_element_type=jnp.float32
    )
    low_rank = (low_rank * selected_experts[:, :, None]).astype(jnp.bfloat16)
    return jnp.einsum("tar,are->te", low_rank, up_weights, preferred_element_type=jnp.float32)


def body(
    tokens,
    lengths,
    prompt_adapter,
    routes,
    routing_weight,
    attention_gain,
    query_weight,
    key_weight,
    value_weight,
    output_weight,
    adapter_down_maps,
    adapter_up_query_output,
    adapter_up_key_value,
    expert_gain,
    gate_weight,
    up_weight,
    down_weight,
    closing_gain,
    vocab_projection,
):
    rows_in = tokens[0]
    tok_count = rows_in.shape[0]
    model_width = rows_in.shape[1]
    prompt_lens = lengths[0]
    owners = prompt_adapter[0]
    ratio = HEADS // KV_HEADS
    logit_scale = HEAD ** (-0.5)
    down_all, wide_all, narrow_all = (
        lax.all_gather(adapter_down_maps, "grp", axis=1, tiled=True),
        lax.all_gather(adapter_up_query_output, "grp", axis=1, tiled=True),
        lax.all_gather(adapter_up_key_value, "grp", axis=1, tiled=True),
    )
    row_index = lax.axis_index("seq") * tok_count + jnp.arange(tok_count, dtype=jnp.int32)
    document, offsets, member = doc_layout(prompt_lens, row_index)
    adapter = jnp.sum(jnp.where(member, owners[None, :], 0), axis=1)
    selected_experts = (
        adapter[:, None] == jnp.arange(down_all.shape[1], dtype=jnp.int32)[None, :]
    ).astype(jnp.float32)
    normalized_rows = rms_scaled(rows_in, attention_gain)
    query_matrix = jnp.dot(
        normalized_rows, query_weight, preferred_element_type=jnp.float32
    ) + adapter_delta(normalized_rows, selected_experts, down_all[0], wide_all[0])
    query_matrix = rotate(query_matrix.reshape(tok_count, HEADS, HEAD), offsets).astype(
        jnp.bfloat16
    )
    query_matrix = query_matrix.reshape(tok_count, KV_HEADS, ratio, HEAD)
    key_matrix = jnp.dot(
        normalized_rows, key_weight, preferred_element_type=jnp.float32
    ) + adapter_delta(normalized_rows, selected_experts, down_all[1], narrow_all[0])
    key_matrix = (
        rotate(key_matrix.reshape(tok_count, KV_HEADS, HEAD), offsets)
        .astype(jnp.bfloat16)
        .reshape(tok_count, KV_HEADS * HEAD)
    )
    value_matrix = (
        jnp.dot(normalized_rows, value_weight, preferred_element_type=jnp.float32)
        + adapter_delta(normalized_rows, selected_experts, down_all[2], narrow_all[1])
    ).astype(jnp.bfloat16)
    running_max = jnp.full((KV_HEADS, ratio, tok_count), MASKED, jnp.float32)
    key_part = lax.all_gather(key_matrix, "seq", axis=0, tiled=True)
    value_part = lax.all_gather(value_matrix, "seq", axis=0, tiled=True)
    key_count = key_part.shape[0]
    key_index = jnp.arange(key_count, dtype=jnp.int32)
    key_doc, _, _ = doc_layout(prompt_lens, key_index)
    allowed = (key_doc[None, :] == document[:, None]) & (key_index[None, :] <= row_index[:, None])
    attention_logits = (
        jnp.einsum(
            "jhlv,phv->hljp",
            query_matrix,
            key_part.reshape(key_count, KV_HEADS, HEAD),
            preferred_element_type=jnp.float32,
        )
        * logit_scale
    )
    attention_logits = jnp.where(allowed[None, None], attention_logits, MASKED)
    new_max = jnp.maximum(running_max, jnp.max(attention_logits, axis=-1))
    weights = jnp.where(allowed[None, None], jnp.exp(attention_logits - new_max[..., None]), 0.0)
    running_sum = jnp.sum(weights, axis=-1)
    weighted_values = jnp.einsum(
        "ukoe,euh->ukoh",
        weights.astype(jnp.bfloat16),
        value_part.reshape(key_count, KV_HEADS, HEAD),
        preferred_element_type=jnp.float32,
    )
    running_max, running_sum, weighted_values = (new_max, running_sum, weighted_values)
    attention_output = (
        (weighted_values / running_sum[..., None])
        .transpose(2, 0, 1, 3)
        .reshape(tok_count, HEADS * HEAD)
        .astype(jnp.bfloat16)
    )
    outside_mask = jnp.dot(
        attention_output, output_weight, preferred_element_type=jnp.float32
    ) + adapter_delta(attention_output, selected_experts, down_all[3], wide_all[1])
    mixed_rows = (rows_in.astype(jnp.float32) + outside_mask).astype(jnp.bfloat16)
    moe_in = rms_scaled(mixed_rows, expert_gain)
    expert_ids = routes[0].reshape(-1)
    flat_weights = routing_weight[0].reshape(-1)
    onehot = (expert_ids[:, None] == jnp.arange(EXPERTS, dtype=jnp.int32)[None, :]).astype(
        jnp.int32
    )
    slot_index = jnp.sum((jnp.cumsum(onehot, axis=0) - onehot) * onehot, axis=1)
    source_row = jnp.arange(expert_ids.shape[0], dtype=jnp.int32) // TOP
    slot_table = (
        jnp.full((EXPERTS * CAP,), tok_count, jnp.int32)
        .at[expert_ids * CAP + slot_index]
        .set(source_row)
        .reshape(EXPERTS, CAP)
    )
    padded = jnp.concatenate([moe_in, jnp.zeros((1, model_width), jnp.bfloat16)], axis=0)
    groups = lax.axis_size("grp")
    slices_here = gate_weight.shape[0]
    outgoing = padded[jnp.repeat(slot_table, 2, axis=0)].reshape(
        groups, slices_here, CAP, model_width
    )
    arrived = lax.all_to_all(outgoing, "grp", split_axis=0, concat_axis=0, tiled=True)
    gate_proj = jnp.einsum(
        "nlcd,ldf->nlcf", arrived, gate_weight, preferred_element_type=jnp.float32
    )
    up_proj = jnp.einsum("nlcd,ldf->nlcf", arrived, up_weight, preferred_element_type=jnp.float32)
    hidden = (jax.nn.silu(gate_proj) * up_proj).astype(jnp.bfloat16)
    halves = jnp.einsum(
        "nlcf,lfd->nlcd", hidden, down_weight, preferred_element_type=jnp.float32
    ).astype(jnp.bfloat16)
    returned = lax.all_to_all(halves, "grp", split_axis=0, concat_axis=0, tiled=True).reshape(
        -1, model_width
    )
    slice_ids = 2 * expert_ids[:, None] + jnp.arange(2, dtype=jnp.int32)[None, :]
    pick_index = slice_ids * CAP + slot_index[:, None]
    picked = returned[pick_index].astype(jnp.float32).reshape(tok_count, TOP * 2, model_width)
    holder = slice_ids // slices_here
    holder_hot = (holder[:, :, None] == jnp.arange(groups, dtype=jnp.int32)[None, None, :]).astype(
        jnp.float32
    )
    holder_hot = (holder_hot * flat_weights[:, None, None]).reshape(tok_count, TOP * 2, groups)
    partial_value = jnp.einsum(
        "tkg,tkd->tgd", holder_hot, picked, precision=lax.Precision.HIGHEST
    ).astype(jnp.bfloat16)
    combined = jnp.sum(partial_value.astype(jnp.float32), axis=1)
    hidden_out = (mixed_rows.astype(jnp.float32) + combined).astype(jnp.bfloat16)
    last_index = jnp.cumsum(prompt_lens) - 1
    selector = (last_index[:, None] == row_index[None, :]).astype(jnp.bfloat16)
    last_rows = jnp.dot(selector, hidden_out, preferred_element_type=jnp.float32)
    last_rows = rms_scaled(last_rows, closing_gain).astype(jnp.float32)
    own_group = (jnp.arange(groups, dtype=jnp.int32) == lax.axis_index("grp")).astype(jnp.float32)
    spread = own_group[:, None, None] * last_rows[None, :, :]
    gathered = lax.psum(spread, ("seq", "grp"))
    final_rows = gathered.reshape(-1, model_width).astype(jnp.bfloat16)
    logits = jnp.dot(final_rows, vocab_projection, preferred_element_type=jnp.float32)
    global_max = lax.pmax(jnp.max(logits, axis=1), ("seq", "grp"))
    global_sum = lax.psum(jnp.sum(jnp.exp(logits - global_max[:, None]), axis=1), ("seq", "grp"))
    log_probs = logits - (global_max + jnp.log(global_sum))[:, None]
    return (hidden_out[None], log_probs)


def solution(mesh):
    placed = (
        P("grp", "seq", None),
        P("grp", None),
        P("grp", None),
        P("grp", "seq", None),
        P("grp", "seq", None),
        P(),
        P(),
        P(),
        P(),
        P(),
        P(None, "grp", None, None),
        P(None, "grp", None, None),
        P(None, "grp", None, None),
        P(),
        P("grp", None, None),
        P("grp", None, None),
        P("grp", None, None),
        P(),
        P(None, ("seq", "grp")),
    )
    return jax.shard_map(
        body,
        mesh=mesh,
        in_specs=placed,
        out_specs=(P("grp", "seq", None), P(None, ("seq", "grp"))),
        check_vma=False,
    )
```

profile of v0, /device:TPU:1, one launch (start us, length us, event | category | flops | bytes accessed | tf_op | source)
XLA Modules:
  0.0 710.5 jit_solution(9158568903717004309)
XLA Ops:
  7.2 0.7 all-gather.5.cloned.1.call-update
  8.0 0.7 all-gather.9.cloned.1.call-update
  8.7 0.8 copy.64
  9.7 0.7 multiply_bitcast_fusion
  10.4 0.8 reduce-window.10
  11.2 0.7 fusion.77
  12.1 22.3 %all_gather.16 = bf16[2,16,16,512]{3,2,1,0:T(8,128)(2,1)S(1)} all-gather(bf16[2,1,16,512]{3,2,1,0:T(8,128)(2,1)} %param.31), channel_id=1, replica_groups=mesh['seq'=8,'grp'=16] {'grp'}, dimensions={1}, use_global_device_ids=true | all-gather | bytes 557056 | tf_op jit(solution)/shard_map/all_gather | solution.py:84
  34.4 11.3 %reduce-window.11 = s32[40,8,128]{2,1,0:T(8,128)S(1)} reduce-window(s32[40,8,128]{2,1,0:T(8,128)S(1)} %fusion.60, s32[]{:T(128)} %constant.32.clone.1), window={size=1x1x128 pad=0_0x0_0x127_0}, to_apply=%region_9.10 | reduce-window | flops 5201920 | bytes 327684 | tf_op jit(solution)/shard_map/reduce-window.1
  46.4 4.3 scatter_custom_fusion
  50.9 0.7 select_reduce_fusion
  51.7 1.2 fusion.43
  53.3 8.4 %all-gather.5.cloned.1.call-done = bf16[4,16,1536,16]{2,3,1,0:T(8,128)(2,1)} async-done(((bf16[4,1,1536,16]{2,3,1,0:T(8,128)(2,1)}), bf16[4,16,1536,16]{2,3,1,0:T(8,128)(2,1)}) %all-gather.5.cloned.1.call-update) | async-done | bytes 3145744 | tf_op jit(solution)/shard_map/all_gather | solution.py:82
  61.7 3.2 fusion.93
  64.9 0.4 fusion.88
  65.6 1.1 convolution_add_fusion.3
  66.7 1.1 copy.56
  67.8 0.7 pad_maximum_fusion
  68.8 1.6 fusion.86
  70.3 35.7 %all-gather.9.cloned.1.call-done = bf16[2,16,16,1536]{3,2,1,0:T(8,128)(2,1)} async-done(((bf16[2,1,16,1536]{3,2,1,0:T(8,128)(2,1)}), bf16[2,16,16,1536]{3,2,1,0:T(8,128)(2,1)}) %all-gather.9.cloned.1.call-update) | async-done | bytes 1572880 | tf_op jit(solution)/shard_map/all_gather | solution.py:83
  106.0 1.4 convolution_bitcast_fusion.1
  107.4 3.2 convolution_add_fusion.1
  110.9 1.6 fusion.84
  112.8 2.5 fusion.33
  115.3 16.3 %all-gather.7.cloned.1.call-done = bf16[1024,512]{0,1:T(8,128)(2,1)} async-done(((bf16[128,512]{0,1:T(8,128)(2,1)}), bf16[1024,512]{0,1:T(8,128)(2,1)}) %all-gather.7.cloned.1.call-update) | async-done | bytes 1048592 | tf_op jit(solution)/shard_map/all_gather | solution.py:113
  131.6 3.1 fusion
  134.8 4.5 copy-done.2
  139.4 3.0 fusion.2
  142.4 15.8 %all-gather.11.cloned.1.call-done = bf16[1024,512]{1,0:T(8,128)(2,1)} async-done(((bf16[128,512]{1,0:T(8,128)(2,1)}), bf16[1024,512]{1,0:T(8,128)(2,1)}) %all-gather.11.cloned.1.call-update) | async-done | bytes 1048592 | tf_op jit(solution)/shard_map/all_gather | solution.py:114
  158.2 2.3 copy.58
  160.5 8.1 %fusion.40 = bf16[128,8,3,64]{0,3,2,1:T(8,128)(2,1)S(1)} fusion(bf16[1024,8,64,1]{0,2,3,1:T(8,128)(2,1)} %bitcast.215, f32[8,1024,128,3]{2,1,3,0:T(8,128)} %copy-done.2, f32[8,3,128]{2,1,0:T(4,128)S(1)} %broadcast_maximum_fusion, pred[128,1024]{0,1:T(8,128)(4,1)S(1)} %fusion.51, f32[128,8,3]{0,2,1:T(4,128)S(1)} %bitcast.233), kind=kOutput, calls=%fused_computation.49 | convolution fusion | flops 418775040 | bytes 14180352 | tf_op jit(solution)/shard_map/ukoe,euh->ukoh/dot_general | solution.py:132
  168.5 0.4 fusion.95
  169.2 3.3 multiply_reduce_fusion
  172.7 11.9 %gather_fusion = bf16[3200,1536]{1,0:T(8,128)(2,1)} fusion(bf16[129,1536]{1,0:T(8,128)(2,1)S(1)} %concatenate.20, s32[4096]{0:T(1024)S(1)} %pad_clamp_fusion), kind=kCustom, calls=%fused_computation | custom fusion | bytes 19673600 | tf_op jit(solution)/shard_map/gather | solution.py:166
  184.5 117.5 %all_to_all.10 = bf16[16,5,40,1536]{3,2,1,0:T(8,128)(2,1)S(1)} all-to-all(bf16[16,5,40,1536]{3,2,1,0:T(8,128)(2,1)} %bitcast.208), channel_id=1, replica_groups=mesh['seq'=8,'grp'=16] {'grp'}, dimensions={0} | all-to-all | bytes 19660800 | tf_op jit(solution)/shard_map/all_to_all | solution.py:169
  302.1 3.8 copy-done.3
  305.8 4.6 fusion.6
  310.5 13.4 %fusion.1 = bf16[16,5,40,1536]{3,2,0,1:T(8,128)(2,1)} fusion(bf16[5,256,1536]{2,1,0:T(8,128)(2,1)} %param.35, f32[5,16,40,256]{3,2,1,0:T(8,128)} %fusion.6, bf16[5,1536,256]{2,1,0:T(8,128)(2,1)} %param.34, bf16[16,5,40,1536]{3,2,1,0:T(8,128)(2,1)} %copy-done.3), kind=kOutput, calls=%fused_computation.8 | convolution fusion | flops 5042995200 | bytes 30801920 | tf_op jit(solution)/shard_map/nlcf,lfd->nlcd/dot_general | solution.py:175
  323.9 8.3 %copy.70 = bf16[16,5,40,1536]{3,2,1,0:T(8,128)(2,1)} copy(bf16[16,5,40,1536]{3,2,0,1:T(8,128)(2,1)} %fusion.1) | data formatting | bytes 19660800 | tf_op jit(solution)/shard_map/convert_element_type | solution.py:177
  332.2 4.9 all-to-all-start.1
  337.1 0.3 compare_select_fusion
  338.2 141.3 %all-to-all-done.1 = bf16[16,5,40,1536]{3,2,1,0:T(8,128)(2,1)} async-done(((bf16[16,5,40,1536]{3,2,1,0:T(8,128)(2,1)}), bf16[16,5,40,1536]{3,2,1,0:T(8,128)(2,1)}, u32[]{:S(2)}, u32[]{:S(2)}) %all-to-all-start.1) | async-done | bytes 9830432 | tf_op jit(solution)/shard_map/all_to_all | solution.py:178
  479.5 18.3 %gather_fusion.1 = bf16[2048,1536]{1,0:T(8,128)(2,1)} fusion(bf16[3200,1536]{1,0:T(8,128)(2,1)} %bitcast.65, s32[2048]{0:T(1024)S(1)} %broadcast_clamp_fusion), kind=kCustom, calls=%fused_computation.1 | custom fusion | bytes 12591104 | tf_op jit(solution)/shard_map/gather | solution.py:183
  497.8 9.2 %convert_reduce_fusion = f32[128,1536]{1,0:T(8,128)S(1)} fusion(bf16[128,16,1536]{2,1,0:T(8,128)(2,1)} %bitcast.209, f32[128,16]{1,0:T(8,128)S(1)} %copy.62, s32[128,16]{1,0:T(8,128)S(1)} %copy.61), kind=kOutput, calls=%fused_computation.4 | convolution fusion | flops 613285888 | bytes 7094272 | tf_op jit(solution)/shard_map/tkg,tkd->tgd/dot_general | solution.py:189
  507.6 66.9 %all-reduce.2 = bf16[16,3,1536]{2,1,0:T(4,128)(2,1)S(1)} all-reduce(f32[16,3,1536]{2,1,0:T(4,128)S(1)} %broadcast_multiply_fusion), channel_id=1, replica_groups=mesh['seq'=8,'grp'=16] {'seq','grp'}, use_global_device_ids=true, to_apply=%region_15.16 | all-reduce | flops 73728 | bytes 442368 | tf_op jit(solution)/shard_map/psum | solution.py:200
  574.7 1.7 fusion.94
  576.4 64.0 %pmax.7 = f32[48]{0:T(128)S(1)} all-reduce(f32[48]{0:T(128)S(1)} %get-tuple-element.22), channel_id=1, replica_groups=mesh['seq'=8,'grp'=16] {'seq','grp'}, use_global_device_ids=true, to_apply=%region_17.18 | all-reduce | flops 48 | bytes 384 | tf_op jit(solution)/shard_map/pmax | solution.py:203
  640.6 62.6 %psum.15 = f32[48]{0:T(128)S(1)} all-reduce(f32[48]{0:T(128)S(1)} %exponential_reduce_fusion), channel_id=1, replica_groups=mesh['seq'=8,'grp'=16] {'seq','grp'}, use_global_device_ids=true, to_apply=%region_19.20 | all-reduce | flops 48 | bytes 384 | tf_op jit(solution)/shard_map/psum | solution.py:204
  703.2 0.7 broadcast_subtract_fusion
  (86 shorter events, 4.9 us)
Async XLA Ops:
  7.2 58.4 %copy-start = (bf16[1536,512]{1,0:T(8,128)(2,1)S(1)}, bf16[1536,512]{1,0:T(8,128)(2,1)}, u32[]{:S(2)}) copy-start(bf16[1536,512]{1,0:T(8,128)(2,1)} %param.26) | copy-start | bytes 4718596
  7.2 57.7 %copy-start.4 = (bf16[1,128,1536]{2,1,0:T(8,128)(2,1)S(1)}, bf16[1,128,1536]{2,1,0:T(8,128)(2,1)}, u32[]{:S(2)}) copy-start(bf16[1,128,1536]{2,1,0:T(8,128)(2,1)} %param.19) | copy-start | bytes 1179652
  7.2 57.7 %copy-start.7 = (f32[1536]{0:T(1024)S(1)}, f32[1536]{0:T(1024)}, u32[]{:S(2)}) copy-start(f32[1536]{0:T(1024)} %param.24) | copy-start | bytes 18436
  7.2 54.5 %all-gather.5.cloned.1.call-start = ((), (), s32[]{:S(2)}) async-start(), calls=%async_computation.2 | async-start | bytes 3342336 | tf_op jit(solution)/shard_map/all_gather | solution.py:82
  7.9 98.1 %all-gather.9.cloned.1.call-start = ((), (), s32[]{:S(2)}) async-start(), calls=%async_computation.4 | async-start | bytes 1671168 | tf_op jit(solution)/shard_map/all_gather | solution.py:83
  8.7 122.9 %all-gather.7.cloned.1.call-start = ((), (), s32[]{:S(2)}) async-start(), calls=%async_computation.3 | async-start | bytes 1179648 | tf_op jit(solution)/shard_map/all_gather | solution.py:113
  68.5 89.7 %all-gather.11.cloned.1.call-start = ((), (), s32[]{:S(2)}) async-start(), calls=%async_computation.5 | async-start | bytes 1179648 | tf_op jit(solution)/shard_map/all_gather | solution.py:114
  134.8 4.6 copy-start.2
  160.5 8.4 %copy-start.5 = (bf16[2,16,16,1536]{3,2,1,0:T(8,128)(2,1)S(1)}, bf16[2,16,16,1536]{3,2,1,0:T(8,128)(2,1)}, u32[]{:S(2)}) copy-start(bf16[2,16,16,1536]{3,2,1,0:T(8,128)(2,1)} %all-gather.9.cloned.1.call-done) | copy-start | bytes 4718596
  168.5 4.0 copy-start.8
  184.5 121.3 %copy-start.11 = (bf16[5,1536,256]{2,1,0:T(8,128)(2,1)S(1)}, bf16[5,1536,256]{2,1,0:T(8,128)(2,1)}, u32[]{:S(2)}) copy-start(bf16[5,1536,256]{2,1,0:T(8,128)(2,1)} %param.33) | copy-start | bytes 11796484
  302.1 3.8 copy-start.3
  332.2 5.8 copy-start.10
  332.2 147.3 %all-to-all-start.1 = ((bf16[16,5,40,1536]{3,2,1,0:T(8,128)(2,1)}), bf16[16,5,40,1536]{3,2,1,0:T(8,128)(2,1)}, u32[]{:S(2)}, u32[]{:S(2)}) async-start(bf16[16,5,40,1536]{3,2,1,0:T(8,128)(2,1)} %copy.70), calls=%async_computation.1 | async-start | bytes 19660800 | tf_op jit(solution)/shard_map/all_to_all | solution.py:178
  497.8 206.1 %copy-start.1 = (bf16[1536,512]{1,0:T(8,128)(2,1)S(1)}, bf16[1536,512]{1,0:T(8,128)(2,1)}, u32[]{:S(2)}) copy-start(bf16[1536,512]{1,0:T(8,128)(2,1)} %param.26) | copy-start | bytes 4718596
  497.8 9.6 %copy-start.9 = (f32[1536]{0:T(1024)S(1)}, f32[1536]{0:T(1024)}, u32[]{:S(2)}) copy-start(f32[1536]{0:T(1024)} %param.36) | copy-start | bytes 18436
  507.1 196.8 %copy-start.6 = (bf16[128,1536]{1,0:T(8,128)(2,1)}, bf16[128,1536]{1,0:T(8,128)(2,1)S(1)}, u32[]{:S(2)}) copy-start(bf16[128,1536]{1,0:T(8,128)(2,1)S(1)} %add_convert_fusion) | copy-start | bytes 1179652
Sparse Core Ops, SparseCore 0:
  10.2 51.4 all-gather.4
  63.8 42.1 all-gather.8
  107.7 23.8 all-gather.6
  133.8 24.3 all-gather.10
where the time goes:
time: 712 us; the launch traced here: 710 us
  blocking collectives  333 us (47%)
  waiting for transfers between devices  219 us (31%)
  local copies, waits for them, and re-layouts  60.3 us (8%)
  matrix products  56.6 us (8%)
  other arithmetic  21.7 us (3%)
  between operations  14.3 us (2%)
    all_to_all x1, waiting for transfers between devices, body(): lax.all_to_all(halves, 'grp', split_axis=0, concat_axis=0, tiled=True)  141 us
    all_to_all x1, blocking collectives, body(): lax.all_to_all(outgoing, 'grp', split_axis=0, concat_axis=0, tiled=True)  118 us
    psum x1, blocking collectives, body(): gathered = lax.psum(spread, ('seq', 'grp'))  66.9 us
    pmax x1, blocking collectives, body(): global_max = lax.pmax(jnp.max(logits, axis=1), ('seq', 'grp'))  64 us
    psum x1, blocking collectives, body(): lax.psum(jnp.sum(jnp.exp(logits - global_max[:, None]), axis=1), ('seq',...  62.6 us
    all_gather x1, waiting for transfers between devices, body(): lax.all_gather(adapter_up_query_output, 'grp', axis=1, tiled=True)  35.7 us
    all_gather x1, blocking collectives, body(): lax.all_gather(adapter_up_key_value, 'grp', axis=1, tiled=True)  22.3 us
    gather x1, local copies, waits for them, and re-layouts, body(): returned[pick_index].astype(jnp.float32)  18.3 us
  transfers between devices with their start and end apart: 5, of which 5 were waited for; matrix products, arithmetic and copies ran while one was open for 7% of the time, Pallas kernels for 0%

commit v1 on v0

--- a/solution.py
+++ b/solution.py
@@ -111,7 +111,12 @@
     ).astype(jnp.bfloat16)
     running_max = jnp.full((KV_HEADS, ratio, tok_count), MASKED, jnp.float32)
     key_part = lax.all_gather(key_matrix, "seq", axis=0, tiled=True)
-    value_part = lax.all_gather(value_matrix, "seq", axis=0, tiled=True)
+    ring = [value_matrix]
+    for hop in range(7):
+        ring.append(lax.ppermute(ring[-1], "seq", [(dev, (dev + 1) % 8) for dev in range(8)]))
+    value_part = jnp.roll(
+        jnp.concatenate(ring[::-1], axis=0), (lax.axis_index("seq") + 1) * ring[0].shape[0], axis=0
+    )
     key_count = key_part.shape[0]
     key_index = jnp.arange(key_count, dtype=jnp.int32)
     key_doc, _, _ = doc_layout(prompt_lens, key_index)

time: 712 us -> 683 us (0.959)
  waiting for transfers between devices: 219 us -> 186 us
  starting transfers between devices: 5.27 us -> 19.1 us
  matrix products: 56.6 us -> 45.3 us
    all_gather x1, waiting for transfers between devices: 35.7 us -> 19.8 us  [body(): lax.all_gather(adapter_up_query_output, 'grp', axis=1, tiled=True)]
    all_gather x1 -> x0, waiting for transfers between devices: 15.8 us -> none  [body(): value_part = lax.all_gather(value_matrix, 'seq', axis=0, tiled=True)]
    ppermute x0 -> x7, starting transfers between devices: none -> 14.2 us  [body(): lax.ppermute(ring[-1], 'seq', [(dev, (dev + 1) % 8) for dev in range(8)])]
    ppermute x0 -> x7, waiting for transfers between devices: none -> 8.49 us  [body(): lax.ppermute(ring[-1], 'seq', [(dev, (dev + 1) % 8) for dev in range(8)])]
    all_gather x1, waiting for transfers between devices: 16.3 us -> 9.15 us  [body(): key_part = lax.all_gather(key_matrix, 'seq', axis=0, tiled=True)]
  transfers between devices with their start and end apart: 5 -> 11, of which waited for: 5 -> 9; matrix products, arithmetic and copies ran while one was open for 7% -> 6% of each run, Pallas kernels for 0% -> 0%
where the time goes in v1:
time: 683 us; the launch traced here: 682 us
  blocking collectives  334 us (49%)
  waiting for transfers between devices  186 us (27%)
  local copies, waits for them, and re-layouts  57.9 us (8%)
  matrix products  45.3 us (7%)
  other arithmetic  24.9 us (4%)
  starting transfers between devices  19.1 us (3%)
  between operations  14.6 us (2%)
    all_to_all x1, waiting for transfers between devices, body(): lax.all_to_all(halves, 'grp', split_axis=0, concat_axis=0, tiled=True)  141 us
    all_to_all x1, blocking collectives, body(): lax.all_to_all(outgoing, 'grp', split_axis=0, concat_axis=0, tiled=True)  118 us
    psum x1, blocking collectives, body(): gathered = lax.psum(spread, ('seq', 'grp'))  68.2 us
    psum x1, blocking collectives, body(): lax.psum(jnp.sum(jnp.exp(logits - global_max[:, None]), axis=1), ('seq',...  64 us
    pmax x1, blocking collectives, body(): global_max = lax.pmax(jnp.max(logits, axis=1), ('seq', 'grp'))  62.5 us
    all_gather x1, blocking collectives, body(): lax.all_gather(adapter_up_key_value, 'grp', axis=1, tiled=True)  22 us
    all_gather x1, waiting for transfers between devices, body(): lax.all_gather(adapter_up_query_output, 'grp', axis=1, tiled=True)  19.8 us
    gather x1, local copies, waits for them, and re-layouts, body(): returned[pick_index].astype(jnp.float32)  18.3 us
  transfers between devices with their start and end apart: 11, of which 9 were waited for; matrix products, arithmetic and copies ran while one was open for 6% of the time, Pallas kernels for 0%

profile of v1, /device:TPU:1, one launch (start us, length us, event | category | flops | bytes accessed | tf_op | source)
XLA Modules:
  0.0 682.1 jit_solution(3298845460203546452)
XLA Ops:
  9.7 1.3 multiply_bitcast_fusion
  13.4 1.2 fusion.43
  15.2 22.0 %all_gather.13 = bf16[2,16,16,512]{3,2,1,0:T(8,128)(2,1)S(1)} all-gather(bf16[2,1,16,512]{3,2,1,0:T(8,128)(2,1)} %param.31), channel_id=1, replica_groups=mesh['seq'=8,'grp'=16] {'grp'}, dimensions={1}, use_global_device_ids=true | all-gather | bytes 557056 | tf_op jit(solution)/shard_map/all_gather | solution.py:84
  37.2 11.3 %reduce-window.11 = s32[40,8,128]{2,1,0:T(8,128)S(1)} reduce-window(s32[40,8,128]{2,1,0:T(8,128)S(1)} %fusion.60, s32[]{:T(128)} %constant.87.clone.1), window={size=1x1x128 pad=0_0x0_0x127_0}, to_apply=%region_9.10 | reduce-window | flops 5201920 | bytes 327684 | tf_op jit(solution)/shard_map/reduce-window.1
  49.3 4.5 scatter_custom_fusion
  55.6 5.9 all-gather.4.cloned.1.call-done
  61.5 2.9 fusion.93
  64.5 1.2 fusion.84
  66.4 2.1 collective-permute-start
  69.2 1.3 collective-permute-done
  70.5 2.4 collective-permute-start.1
  73.5 1.4 collective-permute-done.1
  74.9 2.4 collective-permute-start.2
  78.1 1.4 collective-permute-done.2
  79.5 2.2 collective-permute-start.3
  82.2 2.9 collective-permute-done.3
  85.2 1.0 collective-permute-start.4
  86.2 19.8 %all-gather.8.cloned.1.call-done = bf16[2,16,16,1536]{3,2,1,0:T(8,128)(2,1)} async-done(((bf16[2,1,16,1536]{3,2,1,0:T(8,128)(2,1)}), bf16[2,16,16,1536]{3,2,1,0:T(8,128)(2,1)}) %all-gather.8.cloned.1.call-update) | async-done | bytes 1572880 | tf_op jit(solution)/shard_map/all_gather | solution.py:83
  105.9 1.4 convolution_bitcast_fusion.1
  107.4 2.7 collective-permute-start.5
  110.1 3.2 convolution_add_fusion.1
  113.6 1.2 collective-permute-start.6
  114.8 0.8 subtract_convert_fusion
  115.7 1.4 collective-permute-done.6
  117.1 0.9 constant_dynamic-update-slice_fusion.14
  118.0 0.9 constant_dynamic-update-slice_fusion.13
  119.1 0.9 constant_dynamic-update-slice_fusion.6
  120.0 0.9 constant_dynamic-update-slice_fusion.5
  121.1 1.3 copy.57
  122.4 9.2 %all-gather.6.cloned.1.call-done = bf16[1024,512]{0,1:T(8,128)(2,1)} async-done(((bf16[128,512]{0,1:T(8,128)(2,1)}), bf16[1024,512]{0,1:T(8,128)(2,1)}) %all-gather.6.cloned.1.call-update) | async-done | bytes 1048592 | tf_op jit(solution)/shard_map/all_gather | solution.py:113
  131.6 3.1 fusion
  134.7 3.0 fusion.2
  137.8 3.5 fusion.40
  142.0 0.9 multiply_reduce_fusion
  143.2 11.9 %gather_fusion = bf16[3200,1536]{1,0:T(8,128)(2,1)} fusion(bf16[129,1536]{1,0:T(8,128)(2,1)S(1)} %concatenate.27, s32[4096]{0:T(1024)S(1)} %copy-done.13), kind=kCustom, calls=%fused_computation | custom fusion | bytes 19673600 | tf_op jit(solution)/shard_map/gather | solution.py:171
  155.1 117.5 %all_to_all.10 = bf16[16,5,40,1536]{3,2,1,0:T(8,128)(2,1)S(1)} all-to-all(bf16[16,5,40,1536]{3,2,1,0:T(8,128)(2,1)} %bitcast.208), channel_id=1, replica_groups=mesh['seq'=8,'grp'=16] {'grp'}, dimensions={0} | all-to-all | bytes 19660800 | tf_op jit(solution)/shard_map/all_to_all | solution.py:174
  272.6 3.8 copy-done.2
  276.4 4.7 fusion.6
  281.1 13.3 %fusion.1 = bf16[16,5,40,1536]{3,2,0,1:T(8,128)(2,1)} fusion(bf16[5,256,1536]{2,1,0:T(8,128)(2,1)} %param.35, f32[5,16,40,256]{3,2,1,0:T(8,128)} %fusion.6, bf16[5,1536,256]{2,1,0:T(8,128)(2,1)} %param.34, bf16[16,5,40,1536]{3,2,1,0:T(8,128)(2,1)} %copy-done.2), kind=kOutput, calls=%fused_computation.8 | convolution fusion | flops 5042995200 | bytes 30801920 | tf_op jit(solution)/shard_map/nlcf,lfd->nlcd/dot_general | solution.py:180
  294.4 8.3 %copy.69 = bf16[16,5,40,1536]{3,2,1,0:T(8,128)(2,1)} copy(bf16[16,5,40,1536]{3,2,0,1:T(8,128)(2,1)} %fusion.1) | data formatting | bytes 19660800 | tf_op jit(solution)/shard_map/convert_element_type | solution.py:182
  302.6 4.8 all-to-all-start.1
  308.6 141.3 %all-to-all-done.1 = bf16[16,5,40,1536]{3,2,1,0:T(8,128)(2,1)} async-done(((bf16[16,5,40,1536]{3,2,1,0:T(8,128)(2,1)}), bf16[16,5,40,1536]{3,2,1,0:T(8,128)(2,1)}, u32[]{:S(2)}, u32[]{:S(2)}) %all-to-all-start.1) | async-done | bytes 9830432 | tf_op jit(solution)/shard_map/all_to_all | solution.py:183
  449.9 18.3 %gather_fusion.1 = bf16[2048,1536]{1,0:T(8,128)(2,1)} fusion(bf16[3200,1536]{1,0:T(8,128)(2,1)} %bitcast.65, s32[2048]{0:T(1024)S(1)} %broadcast_clamp_fusion), kind=kCustom, calls=%fused_computation.1 | custom fusion | bytes 12591104 | tf_op jit(solution)/shard_map/gather | solution.py:188
  468.2 9.2 %convert_reduce_fusion = f32[128,1536]{1,0:T(8,128)S(1)} fusion(bf16[128,16,1536]{2,1,0:T(8,128)(2,1)} %bitcast.209, f32[128,16]{1,0:T(8,128)S(1)} %copy.61, s32[128,16]{1,0:T(8,128)S(1)} %copy.60), kind=kOutput, calls=%fused_computation.4 | convolution fusion | flops 613285888 | bytes 7094272 | tf_op jit(solution)/shard_map/tkg,tkd->tgd/dot_general | solution.py:194
  478.1 68.2 %all-reduce.2 = bf16[16,3,1536]{2,1,0:T(4,128)(2,1)S(1)} all-reduce(f32[16,3,1536]{2,1,0:T(4,128)S(1)} %broadcast_multiply_fusion), channel_id=1, replica_groups=mesh['seq'=8,'grp'=16] {'seq','grp'}, use_global_device_ids=true, to_apply=%region_15.16 | all-reduce | flops 73728 | bytes 442368 | tf_op jit(solution)/shard_map/psum | solution.py:205
  546.4 1.7 fusion.94
  548.1 62.5 %pmax.7 = f32[48]{0:T(128)S(1)} all-reduce(f32[48]{0:T(128)S(1)} %get-tuple-element.22), channel_id=1, replica_groups=mesh['seq'=8,'grp'=16] {'seq','grp'}, use_global_device_ids=true, to_apply=%region_17.18 | all-reduce | flops 48 | bytes 384 | tf_op jit(solution)/shard_map/pmax | solution.py:208
  610.8 64.0 %psum.15 = f32[48]{0:T(128)S(1)} all-reduce(f32[48]{0:T(128)S(1)} %exponential_reduce_fusion), channel_id=1, replica_groups=mesh['seq'=8,'grp'=16] {'seq','grp'}, use_global_device_ids=true, to_apply=%region_19.20 | all-reduce | flops 48 | bytes 384 | tf_op jit(solution)/shard_map/psum | solution.py:209
  (159 shorter events, 15.0 us)
Async XLA Ops:
  7.2 58.8 %copy-start = (bf16[1536,512]{1,0:T(8,128)(2,1)S(1)}, bf16[1536,512]{1,0:T(8,128)(2,1)}, u32[]{:S(2)}) copy-start(bf16[1536,512]{1,0:T(8,128)(2,1)} %param.27) | copy-start | bytes 4718596
  7.2 54.3 %all-gather.4.cloned.1.call-start = ((), (), s32[]{:S(2)}) async-start(), calls=%async_computation.2 | async-start | bytes 3342336 | tf_op jit(solution)/shard_map/all_gather | solution.py:82
  7.9 98.0 %all-gather.8.cloned.1.call-start = ((), (), s32[]{:S(2)}) async-start(), calls=%async_computation.4 | async-start | bytes 1671168 | tf_op jit(solution)/shard_map/all_gather | solution.py:83
  8.7 122.9 %all-gather.6.cloned.1.call-start = ((), (), s32[]{:S(2)}) async-start(), calls=%async_computation.3 | async-start | bytes 1179648 | tf_op jit(solution)/shard_map/all_gather | solution.py:113
  9.7 44.1 %copy-start.19 = (s32[1024]{0:T(1024)}, s32[1024]{0:T(1024)S(1)}, u32[]{:S(2)}) copy-start(s32[1024]{0:T(1024)S(1)} %broadcast_in_dim_reshape_squeeze.2) | copy-start | bytes 12292
  11.0 53.5 %copy-start.27 = (s32[128]{0:T(128)}, s32[128]{0:T(128)S(1)}, u32[]{:S(2)}) copy-start(s32[128]{0:T(128)S(1)} %iota_add_fusion) | copy-start | bytes 1540
  11.8 0.8 copy-start.29
  49.2 4.5 copy-start.17
  53.9 10.6 %copy-start.3 = (bf16[1,128,1536]{2,1,0:T(8,128)(2,1)S(1)}, bf16[1,128,1536]{2,1,0:T(8,128)(2,1)}, u32[]{:S(2)}) copy-start(bf16[1,128,1536]{2,1,0:T(8,128)(2,1)} %param.19) | copy-start | bytes 1179652
  53.9 10.6 %copy-start.16 = (f32[1536]{0:T(1024)S(1)}, f32[1536]{0:T(1024)}, u32[]{:S(2)}) copy-start(f32[1536]{0:T(1024)} %param.24) | copy-start | bytes 18436
  61.5 4.4 copy-start.24
  64.5 8.5 %copy-start.4 = (bf16[1536,512]{1,0:T(8,128)(2,1)S(1)}, bf16[1536,512]{1,0:T(8,128)(2,1)}, u32[]{:S(2)}) copy-start(bf16[1536,512]{1,0:T(8,128)(2,1)} %param.26) | copy-start | bytes 4718596
  66.4 11.0 %copy-start.14 = (f32[128,32]{0,1:T(8,128)S(1)}, f32[128,32]{0,1:T(8,128)}, u32[]{:S(2)}) copy-start(f32[128,32]{0,1:T(8,128)} %get-tuple-element.14) | copy-start | bytes 49156
  66.4 11.0 %copy-start.15 = (f32[128,32]{0,1:T(8,128)S(1)}, f32[128,32]{0,1:T(8,128)}, u32[]{:S(2)}) copy-start(f32[128,32]{0,1:T(8,128)} %get-tuple-element.15) | copy-start | bytes 49156
  66.4 15.4 %copy-start.8 = (bf16[1,16,1536,16]{2,3,1,0:T(8,128)(2,1)S(1)}, bf16[1,16,1536,16]{2,3,1,0:T(8,128)(2,1)}, u32[]{:S(2)}) copy-start(bf16[1,16,1536,16]{2,3,1,0:T(8,128)(2,1)} %get-tuple-element.4) | copy-start | bytes 2359300
  66.4 15.3 %copy-start.25 = (f32[128]{0:T(128)S(1)}, f32[128]{0:T(128)}, u32[]{:S(2)}) copy-start(f32[128]{0:T(128)} %add_rsqrt_fusion.2) | copy-start | bytes 1540
  66.4 4.1 collective-permute-start
  70.5 36.8 %copy-start.9 = (bf16[128,512]{1,0:T(8,128)(2,1)}, bf16[128,512]{1,0:T(8,128)(2,1)S(1)}, u32[]{:S(2)}) copy-start(bf16[128,512]{1,0:T(8,128)(2,1)S(1)} %collective-permute-done) | copy-start | bytes 393220
  70.5 4.4 collective-permute-start.1
  74.9 32.5 %copy-start.11 = (bf16[128,512]{1,0:T(8,128)(2,1)}, bf16[128,512]{1,0:T(8,128)(2,1)S(1)}, u32[]{:S(2)}) copy-start(bf16[128,512]{1,0:T(8,128)(2,1)S(1)} %collective-permute-done.1) | copy-start | bytes 393220
  74.9 4.6 collective-permute-start.2
  79.5 5.6 collective-permute-start.3
  85.2 22.2 %collective-permute-start.4 = (bf16[128,512]{1,0:T(8,128)(2,1)S(1)}, bf16[128,512]{1,0:T(8,128)(2,1)}, u32[]{:S(2)}, u32[]{:S(2)}) collective-permute-start(bf16[128,512]{1,0:T(8,128)(2,1)S(1)} %collective-permute-done.3), channel_id=1, source_target_pairs={{0,16},{16,32},{32,48},{48,64},{64,80},{80,96},{96,112},{112,0},{1... | collective-permute-start | bytes 393224 | tf_op jit(solution)/shard_map/ppermute | solution.py:116
  107.4 6.2 collective-permute-start.5
  113.3 5.7 copy-start.12
  113.3 5.7 copy-start.10
  113.6 3.5 collective-permute-start.6
  134.7 3.1 copy-start.7
  137.8 4.2 slice-start
  137.8 3.9 copy-start.5
  137.8 4.2 slice-start.1
  142.0 1.0 copy-start.22
  142.0 1.1 copy-start.13
  155.1 121.3 %copy-start.31 = (bf16[5,1536,256]{2,1,0:T(8,128)(2,1)S(1)}, bf16[5,1536,256]{2,1,0:T(8,128)(2,1)}, u32[]{:S(2)}) copy-start(bf16[5,1536,256]{2,1,0:T(8,128)(2,1)} %param.33) | copy-start | bytes 11796484
  272.6 3.8 copy-start.2
  302.6 4.8 copy-start.20
  302.6 4.9 copy-start.18
  302.6 5.6 copy-start.21
  302.6 5.8 copy-start.26
  302.6 5.9 copy-start.30
  302.6 147.2 %all-to-all-start.1 = ((bf16[16,5,40,1536]{3,2,1,0:T(8,128)(2,1)}), bf16[16,5,40,1536]{3,2,1,0:T(8,128)(2,1)}, u32[]{:S(2)}, u32[]{:S(2)}) async-start(bf16[16,5,40,1536]{3,2,1,0:T(8,128)(2,1)} %copy.69), calls=%async_computation.1 | async-start | bytes 19660800 | tf_op jit(solution)/shard_map/all_to_all | solution.py:183
  468.2 9.3 %copy-start.28 = (s32[128]{0:T(128)S(1)}, s32[128]{0:T(128)}, u32[]{:S(2)}) copy-start(s32[128]{0:T(128)} %copy-done.27) | copy-start | bytes 1540
  468.2 9.6 %copy-start.23 = (f32[1536]{0:T(1024)S(1)}, f32[1536]{0:T(1024)}, u32[]{:S(2)}) copy-start(f32[1536]{0:T(1024)} %param.36) | copy-start | bytes 18436
  468.2 207.3 %copy-start.1 = (bf16[1536,512]{1,0:T(8,128)(2,1)S(1)}, bf16[1536,512]{1,0:T(8,128)(2,1)}, u32[]{:S(2)}) copy-start(bf16[1536,512]{1,0:T(8,128)(2,1)} %param.27) | copy-start | bytes 4718596
  477.5 198.1 %copy-start.6 = (bf16[128,1536]{1,0:T(8,128)(2,1)}, bf16[128,1536]{1,0:T(8,128)(2,1)S(1)}, u32[]{:S(2)}) copy-start(bf16[128,1536]{1,0:T(8,128)(2,1)S(1)} %add_convert_fusion) | copy-start | bytes 1179652
Sparse Core Ops, SparseCore 0:
  10.2 51.3 all-gather.3
  63.7 42.2 all-gather.7
  107.6 23.8 all-gather.5
